TPU v7x, 128 devices: a whole 4x4x4 slice. The times are simulated.
128 devices in a mesh: row: 16 (over x, y_lo, core), col: 8 (over y_hi, z).
Axes of the slice: x: 4, y: 4 (y_hi: 2, y_lo: 2; y = y_hi * 2 + y_lo), z: 4, core: 2. Of those that a mesh axis runs over, the one named last changes fastest.
Arguments:
- weight: bfloat16 [6144, 6144], P('row', 'col'), may hold values from -6 to 6
- right_op: bfloat16 [8192, 6144], P('row', 'col'), may hold values from -0.078125 to 0.078125
- left_op: bfloat16 [8192, 6144], P('row', 'col'), may hold values from -0.078125 to 0.078125
Outputs:
- grown: bfloat16 [8192, 8192], P(('row', 'col'))
All inputs are finite; a program needn't handle non-finite values.
Results may differ from a plain program's by a relative error of at most 0.018.
Values may be sent and summed in bfloat16 or wider, within the bound.
No kernel may reach another device: no remote copies, remote signals or barrier semaphores. Data moves between devices by JAX's collectives and lax.ppermute only.
A program may use at most 64 MiB of HBM per device.

v0:
```python
import jax
import jax.numpy as jnp
from jax import lax
from jax.sharding import PartitionSpec as P


def split_up(x, dim, size):
    shape = x.shape
    pieces = x.reshape(*shape[:dim], size, shape[dim] // size, *shape[dim + 1 :])
    return jnp.moveaxis(pieces, dim, 0)


def sum_at_owner(x, axis, dim):
    size = lax.axis_size(axis)
    pieces = lax.all_to_all(split_up(x, dim, size), axis, 0, 0, tiled=True)
    return jnp.sum(pieces.astype(jnp.float32), axis=0)


def round_terms(values):
    return lax.optimization_barrier(values.astype(jnp.bfloat16)).astype(jnp.float32)


def shards(weight, right_op, left_op):
    weight_whole = lax.all_gather(weight, "row", axis=0, tiled=True)
    partial_value = jnp.einsum(
        "ik,jk->ij", weight_whole, right_op, preferred_element_type=jnp.float32
    )
    middle = sum_at_owner(round_terms(partial_value).astype(jnp.bfloat16), "col", 0).astype(
        jnp.bfloat16
    )
    terms = jnp.dot(
        left_op,
        lax.all_gather(middle, "row", axis=1, tiled=True),
        preferred_element_type=jnp.float32,
    )
    return lax.psum_scatter(
        round_terms(terms).astype(jnp.bfloat16), "col", scatter_dimension=0, tiled=True
    )


def solution(mesh):
    in_specs = (P("row", "col"), P("row", "col"), P("row", "col"))
    out_specs = P(("row", "col"), None)
    return jax.shard_map(shards, mesh=mesh, in_specs=in_specs, out_specs=out_specs, check_vma=False)
```

profile of v0, /device:TPU:0, one launch (start us, length us, event | category | flops | bytes accessed | tf_op | source)
XLA Modules:
  0.0 379.2 jit_solution(7308006104932658179)
XLA Ops:
  6.5 0.0 copy-start
  6.5 0.0 all-gather.3.cloned.1.call-start
  6.5 0.7 all-gather.3.cloned.1.call-update
  7.3 0.0 all-gather.5.cloned.1.call-start
  7.3 61.2 %all-gather.3.cloned.1.call-done = bf16[6144,768]{1,0:T(8,128)(2,1)} async-done(((bf16[384,768]{1,0:T(8,128)(2,1)}), bf16[6144,768]{1,0:T(8,128)(2,1)}) %all-gather.3.cloned.1.call-update) | async-done | bytes 9437200 | tf_op jit(solution)/shard_map/all_gather | solution.py:24
  68.5 9.2 %convolution_convert_fusion.1 = bf16[6144,512]{1,0:T(8,128)(2,1)S(1)} fusion(bf16[6144,768]{1,0:T(8,128)(2,1)} %all-gather.3.cloned.1.call-done, bf16[512,768]{1,0:T(8,128)(2,1)} %param.4), kind=kOutput, calls=%fused_computation.2 | convolution fusion | flops 4834983936 | bytes 16515072 | tf_op jit(solution)/shard_map/ik,jk->ij/dot_general | solution.py:25
  77.7 80.4 %all_to_all.5 = bf16[8,768,512]{2,1,0:T(8,128)(2,1)} all-to-all(bf16[8,768,512]{2,1,0:T(8,128)(2,1)S(1)} %bitcast.8), channel_id=1, replica_groups=mesh['row'=16,'col'=8] {'col'}, dimensions={0} | all-to-all | bytes 12582912 | tf_op jit(solution)/shard_map/all_to_all | solution.py:15
  158.1 4.8 %reduce_sum.12 = bf16[768,512]{1,0:T(8,128)(2,1)} reduce(bf16[8,768,512]{2,1,0:T(8,128)(2,1)} %all_to_all.5, bf16[]{:T(256)} %constant.2.clone.1), dimensions={0}, to_apply=%region_0.0 | reduce | flops 2752512 | bytes 7077890 | tf_op jit(solution)/shard_map/reduce_sum | solution.py:16
  162.9 0.0 all-gather.5.cloned.1.call-update
  162.9 0.0 reduce-scatter.4.cloned.1.call-start
  163.0 68.8 %all-gather.5.cloned.1.call-done = bf16[768,8192]{1,0:T(8,128)(2,1)} async-done(((bf16[768,512]{1,0:T(8,128)(2,1)}), bf16[768,8192]{1,0:T(8,128)(2,1)}) %all-gather.5.cloned.1.call-update) | async-done | bytes 12582928 | tf_op jit(solution)/shard_map/all_gather | solution.py:33
  231.7 0.0 copy-done
  231.7 13.6 %fusion = bf16[512,8192]{0,1:T(8,128)(2,1)} fusion(bf16[768,8192]{1,0:T(8,128)(2,1)} %all-gather.5.cloned.1.call-done, bf16[512,768]{1,0:T(8,128)(2,1)S(1)} %copy-done), kind=kOutput, calls=%fused_computation.1 | convolution fusion | flops 6446645248 | bytes 21757952 | tf_op jit(solution)/shard_map/dot_general | solution.py:31
  245.4 11.9 %copy.6 = bf16[512,8192]{1,0:T(8,128)(2,1)} copy(bf16[512,8192]{0,1:T(8,128)(2,1)} %fusion) | data formatting | bytes 16777216
  257.2 0.0 reduce-scatter.4.cloned.1.call-update
  257.3 115.4 %reduce-scatter.4.cloned.1.call-done = bf16[64,8192]{1,0:T(8,128)(2,1)} async-done(((bf16[512,8192]{1,0:T(8,128)(2,1)}), bf16[64,8192]{1,0:T(8,128)(2,1)}) %reduce-scatter.4.cloned.1.call-update) | async-done | bytes 1048592 | tf_op jit(solution)/shard_map/reduce_scatter | solution.py:36
Async XLA Ops:
  6.5 225.2 %copy-start = (bf16[512,768]{1,0:T(8,128)(2,1)S(1)}, bf16[512,768]{1,0:T(8,128)(2,1)}, u32[]{:S(2)}) copy-start(bf16[512,768]{1,0:T(8,128)(2,1)} %param.5) | copy-start | bytes 2359300
  6.5 62.0 %all-gather.3.cloned.1.call-start = ((), (), s32[]{:S(2)}) async-start(), calls=%async_computation.2 | async-start | bytes 10027008 | tf_op jit(solution)/shard_map/all_gather | solution.py:24
  7.3 224.5 %all-gather.5.cloned.1.call-start = ((), (), s32[]{:S(2)}) async-start(), calls=%async_computation.3 | async-start | bytes 13369344 | tf_op jit(solution)/shard_map/all_gather | solution.py:33
  162.9 209.8 %reduce-scatter.4.cloned.1.call-start = ((), (), s32[]{:S(2)}) async-start(), calls=%async_computation.4 | async-start | bytes 9437184 | tf_op jit(solution)/shard_map/reduce_scatter | solution.py:36
Sparse Core Ops, SparseCore 0:
  9.0 59.4 all-gather.2
  163.0 68.6 all-gather.4
  257.4 115.2 reduce-scatter.3
where the time goes:
time: 380 us; the launch traced here: 379 us
  waiting for transfers between devices  246 us (65%)
  blocking collectives  80.4 us (21%)
  matrix products  22.8 us (6%)
  between operations  13.1 us (3%)
  local copies, waits for them, and re-layouts  11.9 us (3%)
  other arithmetic  4.79 us (1%)
    reduce_scatter x1, waiting for transfers between devices, shards(): lax.psum_scatter(round_terms(terms).astype(jnp.bfloat16), 'col', scatter_...  115 us
    all_to_all x1, blocking collectives, sum_at_owner(): pieces = lax.all_to_all(split_up(x, dim, size), axis, 0, 0, tiled=True)  80.4 us
    all_gather x1, waiting for transfers between devices, shards(): lax.all_gather(middle, 'row', axis=1, tiled=True)  68.8 us
    all_gather x1, waiting for transfers between devices, shards(): weight_whole = lax.all_gather(weight, 'row', axis=0, tiled=True)  61.2 us
    dot_general x1, matrix products, shards(): jnp.dot(left_op, lax.all_gather(middle, 'row', axis=1, tiled=True), prefe...  13.6 us
    unnamed x3, local copies, waits for them, and re-layouts  11.9 us
    dot_general x1, matrix products, shards(): jnp.einsum('ik,jk->ij', weight_whole, right_op, preferred_element_type=jn...  9.17 us
  transfers between devices with their start and end apart: 3, of which 3 were waited for; matrix products, arithmetic and copies ran while one was open for 0% of the time, Pallas kernels for 0%

commit v1 on v0

--- a/solution.py
+++ b/solution.py
@@ -30,7 +30,9 @@
     )
     terms = jnp.dot(
         left_op,
-        lax.all_gather(middle, "row", axis=1, tiled=True),
+        jnp.concatenate(
+            lax.all_to_all(jnp.stack([middle] * lax.axis_size("row")), "row", 0, 0), axis=1
+        ),
         preferred_element_type=jnp.float32,
     )
     return lax.psum_scatter(

time: 380 us -> 452 us (1.19)
  blocking collectives: 80.4 us -> 225 us
  waiting for transfers between devices: 246 us -> 173 us
  local copies, waits for them, and re-layouts: 11.9 us -> 18.1 us
    all_to_all x0 -> x1, blocking collectives: none -> 144 us  [shards(): lax.all_to_all(jnp.stack([middle] * lax.axis_size('row')), 'row', 0, 0)]
    all_gather x1 -> x0, waiting for transfers between devices: 68.8 us -> none  [shards(): lax.all_gather(middle, 'row', axis=1, tiled=True)]
    another operation x0 -> x1, local copies, waits for them, and re-layouts: none -> 5.78 us  [shards(): jnp.stack([middle] * lax.axis_size('row'))]
  transfers between devices with their start and end apart: 3 -> 2, of which waited for: 3 -> 2; matrix products, arithmetic and copies ran while one was open for 0% -> 0% of each run, Pallas kernels for 0% -> 0%
where the time goes in v1:
time: 452 us
  blocking collectives  225 us (50%)
  waiting for transfers between devices  173 us (38%)
  matrix products  18.3 us (4%)
  local copies, waits for them, and re-layouts  18.1 us (4%)
  between operations  13.4 us (3%)
    all_to_all x1, blocking collectives, shards(): lax.all_to_all(jnp.stack([middle] * lax.axis_size('row')), 'row', 0, 0)  144 us
    reduce_scatter x1, waiting for transfers between devices, shards(): lax.psum_scatter(round_terms(terms).astype(jnp.bfloat16), 'col', scatter_...  111 us
    all_to_all x1, blocking collectives, sum_at_owner(): pieces = lax.all_to_all(split_up(x, dim, size), axis, 0, 0, tiled=True)  80.4 us
    all_gather x1, waiting for transfers between devices, shards(): weight_whole = lax.all_gather(weight, 'row', axis=0, tiled=True)  61.2 us
    unnamed x3, local copies, waits for them, and re-layouts  12 us
    dot_general x1, matrix products, shards(): jnp.einsum('ik,jk->ij', weight_whole, right_op, preferred_element_type=jn...  9.17 us
    dot_general x1, matrix products, shards(): jnp.dot(left_op, jnp.concatenate(lax.all_to_all(jnp.stack([middle] * lax....  9.15 us
  transfers between devices with their start and end apart: 2, of which 2 were waited for; matrix products, arithmetic and copies ran while one was open for 0% of the time, Pallas kernels for 0%

profile of v1, /device:TPU:0, one launch (start us, length us, event | category | flops | bytes accessed | tf_op | source)
XLA Modules:
  0.0 451.8 jit_solution(13155819684709232751)
XLA Ops:
  6.5 0.0 copy-start
  6.5 0.0 all-gather.2.cloned.1.call-start
  6.5 0.7 all-gather.2.cloned.1.call-update
  7.3 0.0 reduce-scatter.4.cloned.1.call-start
  7.3 61.2 %all-gather.2.cloned.1.call-done = bf16[6144,768]{1,0:T(8,128)(2,1)} async-done(((bf16[384,768]{1,0:T(8,128)(2,1)}), bf16[6144,768]{1,0:T(8,128)(2,1)}) %all-gather.2.cloned.1.call-update) | async-done | bytes 9437200 | tf_op jit(solution)/shard_map/all_gather | solution.py:24
  68.5 9.2 %convolution_convert_fusion.1 = bf16[6144,512]{1,0:T(8,128)(2,1)S(1)} fusion(bf16[6144,768]{1,0:T(8,128)(2,1)} %all-gather.2.cloned.1.call-done, bf16[512,768]{1,0:T(8,128)(2,1)} %param.4), kind=kOutput, calls=%fused_computation.2 | convolution fusion | flops 4834983936 | bytes 16515072 | tf_op jit(solution)/shard_map/ik,jk->ij/dot_general | solution.py:25
  77.7 80.4 %all_to_all.10 = bf16[8,768,512]{2,1,0:T(8,128)(2,1)} all-to-all(bf16[8,768,512]{2,1,0:T(8,128)(2,1)S(1)} %bitcast.12), channel_id=1, replica_groups=mesh['row'=16,'col'=8] {'col'}, dimensions={0} | all-to-all | bytes 12582912 | tf_op jit(solution)/shard_map/all_to_all | solution.py:15
  158.1 4.2 reduce_sum.12
  162.2 0.3 copy.6
  162.5 5.8 %stack.2 = bf16[16,768,512]{1,2,0:T(8,128)(2,1)} broadcast(bf16[768,512]{0,1:T(8,128)(2,1)S(1)} %copy.6), dimensions={1,2} | broadcast | bytes 13369344 | tf_op jit(solution)/shard_map/stack | solution.py:34
  168.3 144.2 %all_to_all.11 = bf16[16,768,512]{1,2,0:T(8,128)(2,1)S(1)} all-to-all(bf16[16,768,512]{1,2,0:T(8,128)(2,1)} %stack.2), channel_id=1, replica_groups=mesh['row'=16,'col'=8] {'row'}, dimensions={0} | all-to-all | bytes 25165824 | tf_op jit(solution)/shard_map/all_to_all | solution.py:34
  312.5 0.0 copy-done
  312.5 9.2 %fusion = bf16[512,8192]{0,1:T(8,128)(2,1)} fusion(bf16[768,8192]{0,1:T(8,128)(2,1)S(1)} %bitcast.11, bf16[512,768]{1,0:T(8,128)(2,1)S(1)} %copy-done), kind=kOutput, calls=%fused_computation.1 | convolution fusion | flops 6446645248 | bytes 21757952 | tf_op jit(solution)/shard_map/dot_general | solution.py:31
  321.7 12.0 %copy.8 = bf16[512,8192]{1,0:T(8,128)(2,1)} copy(bf16[512,8192]{0,1:T(8,128)(2,1)} %fusion) | data formatting | bytes 16777216
  333.7 0.0 reduce-scatter.4.cloned.1.call-update
  333.7 111.2 %reduce-scatter.4.cloned.1.call-done = bf16[64,8192]{1,0:T(8,128)(2,1)} async-done(((bf16[512,8192]{1,0:T(8,128)(2,1)}), bf16[64,8192]{1,0:T(8,128)(2,1)}) %reduce-scatter.4.cloned.1.call-update) | async-done | bytes 1048592 | tf_op jit(solution)/shard_map/reduce_scatter | solution.py:38
Async XLA Ops:
  6.5 306.0 %copy-start = (bf16[512,768]{1,0:T(8,128)(2,1)S(1)}, bf16[512,768]{1,0:T(8,128)(2,1)}, u32[]{:S(2)}) copy-start(bf16[512,768]{1,0:T(8,128)(2,1)} %param.5) | copy-start | bytes 2359300
  6.5 62.0 %all-gather.2.cloned.1.call-start = ((), (), s32[]{:S(2)}) async-start(), calls=%async_computation.3 | async-start | bytes 10027008 | tf_op jit(solution)/shard_map/all_gather | solution.py:24
  7.3 437.7 %reduce-scatter.4.cloned.1.call-start = ((), (), s32[]{:S(2)}) async-start(), calls=%async_computation.4 | async-start | bytes 9437184 | tf_op jit(solution)/shard_map/reduce_scatter | solution.py:38
Sparse Core Ops, SparseCore 0:
  9.0 59.4 all-gather.1
  333.9 111.0 reduce-scatter.3
